TPU v7x, 32 devices: a whole 2x2x4 slice. The times are simulated.
32 devices in a mesh: comp: 4 (over y, core), tile: 8 (over z, x).
Axes of the slice: x: 2, y: 2, z: 4, core: 2. Of those that a mesh axis runs over, the one named last changes fastest.
Arguments:
- state: float32 [2, 8, 256, 4096], P(None, None, 'comp', 'tile'), may hold values from -6 to 6
- courant: float32 [8, 256], P(None, 'comp'), may hold values from -0.9 to 0.9
- mixing: float32 [7, 256], P(None, 'comp'), may hold values from 0.05 to 0.24
- exchange_coef: float32 [256, 4096], P('comp', 'tile'), may hold values from 0.2 to 0.8
- sea_mask: int32 [256, 4096], P('comp', 'tile'), may hold values 0 or 1
- margin_count: int32 [4, 8, 3, 4], P('comp', 'tile'), may hold values from 0 to 4096, as said below
- margin_row: int32 [4, 8, 3, 4, 4096], P('comp', 'tile'), may hold values from 0 to 63
- margin_col: int32 [4, 8, 3, 4, 4096], P('comp', 'tile'), may hold values from 0 to 511, as said below
- margin_weight: float32 [4, 8, 3, 4, 4096], P('comp', 'tile'), may hold values from 0.05 to 0.6
Outputs:
- new_state: float32 [2, 8, 256, 4096], P(None, None, 'comp', 'tile')
- partner_surface: float32 [2, 256, 4096], P(None, 'comp', 'tile')
Inputs may be any that keep to these rules, and one draw needn't show every extreme that they name: margin_count[g, t, o, h] equals margin_count[h, (t + o - 1) mod 8, 2 - o, g], and row r of the one list is the same margin as row r of the other. Only pairs of one atmosphere device (comp index below 3) and one ocean device have rows: an atmosphere device couples with the three ocean devices at tile offsets -1, 0 and 1, an ocean device with the atmosphere devices at those offsets; every such pair has at least 3584 rows. `margin_col`: for list index o = 0 (partner to the west) the columns lie below 128, for o = 2 (partner to the east) at 384 or above.
All inputs are finite; a program needn't handle non-finite values. No bound on the sum of `sea_mask` on one device may be relied on, other than what follows from the above.
Results may differ from a plain program's by a relative error of at most 0.0003.
Values sent between devices are 32-bit elements; how exact they have to be, the bound alone decides.
A program may use at most 64 MiB of HBM per device.

v0:
```python
import jax
import jax.numpy as jnp
from jax import lax
from jax.sharding import PartitionSpec as P

SUBSTEPS = 2


def with_halo(block, sides, width):
    for axis, dim in sides:
        count = lax.axis_size(axis)
        forward = [(i, i + 1) for i in range(count - 1)]
        forward.append((count - 1, 0))
        backward = [(target, source) for source, target in forward]
        low = lax.ppermute(
            lax.slice_in_dim(block, block.shape[dim] - width, None, axis=dim), axis, forward
        )
        high = lax.ppermute(lax.slice_in_dim(block, 0, width, axis=dim), axis, backward)
        block = jnp.concatenate([low, block, high], axis=dim)
    return block


def transport(padded, speed):
    left = padded[..., :-2]
    middle = padded[..., 1:-1]
    right = padded[..., 2:]
    return (
        middle - 0.5 * speed * (right - left) + 0.5 * speed * speed * (right - 2.0 * middle + left)
    )


def vertical_mix(field, coeff):
    jump_up = field[:, 1:] - field[:, :-1]
    flux = coeff[None, :, :, None] * jump_up
    empty = jnp.zeros_like(flux[:, :1])
    upper = jnp.concatenate([flux, empty], axis=1)
    lower = jnp.concatenate([empty, flux], axis=1)
    return field + upper - lower


def shards(
    state,
    courant,
    mixing,
    exchange_coef,
    sea_mask,
    margin_count,
    margin_row,
    margin_col,
    margin_weight,
):
    field_count, level_count, row_count, col_count = state.shape
    slot_count = margin_row.shape[-1]
    comp_peers = margin_row.shape[3]
    list_count = 3 * comp_peers
    tile_total = lax.axis_size("tile")
    tile_here = lax.axis_index("tile")
    surface_rows = state[:, 0].reshape(field_count * row_count, col_count)
    row_lists = margin_row.reshape(list_count, slot_count)
    col_lists = margin_col.reshape(list_count, slot_count)
    counts = margin_count.reshape(list_count)
    row_iota = jnp.arange(row_count, dtype=jnp.int32)[:, None]
    col_iota = jnp.arange(col_count, dtype=jnp.int32)[:, None]
    slot_iota = jnp.arange(slot_count, dtype=jnp.int32)

    def pick_list(carry, parts):
        row_list, col_list, count_one = parts
        col_table = (col_iota == col_list[None, :]).astype(jnp.float32)
        picked = jnp.dot(
            surface_rows,
            col_table,
            precision=lax.Precision.HIGHEST,
            preferred_element_type=jnp.float32,
        )
        picked = picked.reshape(field_count, row_count, slot_count)
        row_match = row_iota == row_list[None, :]
        values = jnp.sum(jnp.where(row_match[None], picked, 0.0), axis=1)
        values = jnp.where((slot_iota < count_one)[None, :], values, 0.0)
        return (carry, values)

    unused, picked_all = lax.scan(pick_list, 0, (row_lists, col_lists, counts))
    outgoing = jnp.transpose(
        picked_all.reshape(3, comp_peers, field_count, slot_count), (2, 0, 1, 3)
    )
    partner_tiles = (tile_here + jnp.arange(3, dtype=jnp.int32) - 1) % tile_total
    tile_table = partner_tiles[:, None] == jnp.arange(tile_total, dtype=jnp.int32)[None, :]
    spread = jnp.where(tile_table[None, :, None, :, None], outgoing[:, :, :, None, :], 0.0)
    blocks = jnp.sum(spread, axis=1).reshape(field_count, comp_peers * tile_total, slot_count)
    arrived = lax.all_to_all(blocks, ("comp", "tile"), split_axis=1, concat_axis=1, tiled=True)
    arrived = arrived.reshape(field_count, comp_peers, tile_total, slot_count)
    chosen = jnp.where(tile_table[None, :, None, :, None], arrived[:, None], 0.0)
    incoming = jnp.sum(chosen, axis=3)
    speed = courant[:, :, None]
    field = state
    padded = with_halo(field, (("tile", 3),), SUBSTEPS)
    for step in range(SUBSTEPS):
        padded = vertical_mix(transport(padded, speed), mixing)
    field = padded
    weights = margin_weight.reshape(3, comp_peers, slot_count)
    terms = jnp.transpose(
        (incoming * weights[None]).reshape(field_count, list_count, slot_count), (1, 0, 2)
    )

    def land_list(total, parts):
        row_list, col_list, term_one = parts
        col_table = (col_iota == col_list[None, :]).astype(jnp.float32)
        row_match = row_iota == row_list[None, :]
        spread = jnp.where(row_match[None], term_one[:, None, :], 0.0).reshape(
            field_count * row_count, slot_count
        )
        landed = lax.dot_general(
            spread,
            col_table,
            (((1,), (1,)), ((), ())),
            precision=lax.Precision.HIGHEST,
            preferred_element_type=jnp.float32,
        )
        return (total + landed, 0)

    start_total = jnp.zeros((field_count * row_count, col_count), jnp.float32)
    partner, unused_two = lax.scan(land_list, start_total, (row_lists, col_lists, terms))
    partner = partner.reshape(field_count, row_count, col_count)
    ocean = lax.axis_index("comp") == lax.axis_size("comp") - 1
    rate = exchange_coef * sea_mask.astype(jnp.float32)
    first_own = field[0, 0]
    second_own = field[1, 0]
    first_far = partner[0]
    second_far = partner[1]
    new_first = first_own + rate * (first_far - first_own)
    air_second = second_own + rate * (1.2 * first_far - 0.3 * second_far - second_own)
    sea_second = second_own + rate * (1.2 * first_own - second_far)
    new_second = jnp.where(ocean, sea_second, air_second)
    field = field.at[:, 0].set(jnp.stack([new_first, new_second]))
    return (field, partner)


def solution(mesh):
    in_specs = (
        P(None, None, "comp", "tile"),
        P(None, "comp"),
        P(None, "comp"),
        P("comp", "tile"),
        P("comp", "tile"),
        P("comp", "tile", None, None),
        P("comp", "tile", None, None, None),
        P("comp", "tile", None, None, None),
        P("comp", "tile", None, None, None),
    )
    out_specs = (P(None, None, "comp", "tile"), P(None, "comp", "tile"))
    return jax.shard_map(shards, mesh=mesh, in_specs=in_specs, out_specs=out_specs, check_vma=False)
```

profile of v0, /device:TPU:0, one launch (start us, length us, event | category | flops | bytes accessed | tf_op | source)
XLA Modules:
  0.0 178.6 jit_solution(16265510379821095748)
XLA Ops:
  0.7 2.4 %fusion.21 = (f32[2,8,64,2]{3,2,1,0:T(8,128)}, f32[2,8,64,2]{3,2,1,0:T(8,128)}) fusion(f32[2,8,64,512]{3,2,1,0:T(8,128)} %param.15), kind=kLoop, calls=%fused_computation.54 | loop fusion | bytes 32768 | tf_op jit(solution)/shard_map/slice | solution.py:16
  3.1 6.0 %collective-permute-start.1 = (f32[2,8,64,2]{3,2,1,0:T(8,128)}, f32[2,8,64,2]{3,2,1,0:T(8,128)}, u32[]{:S(2)}, u32[]{:S(2)}) collective-permute-start(f32[2,8,64,2]{3,2,1,0:T(8,128)} %get-tuple-element.167), channel_id=1, source_target_pairs={{1,0},{2,1},{3,2},{4,3},{5,4},{6,5},{7,6},{0,7},{9,8},{10,9},{11,1... | collective-permute-start | bytes 24584 | tf_op jit(solution)/shard_map/ppermute | solution.py:18
  9.4 54.5 %while.23 = (s32[]{:T(128)}, f32[12,2,4096]{2,1,0:T(2,128)S(1)}, s32[12]{0:T(128)S(1)}, s32[12,4096]{1,0:T(8,128)S(1)}, s32[12,4096]{1,0:T(8,128)S(1)}, /*index=5*/f32[128,512]{1,0:T(8,128)S(1)}, s32[]{:T(128)}) while((s32[]{:T(128)}, f32[12,2,4096]{2,1,0:T(2,128)S(1)}, s32[12]{0:T(128)S(1)}, s32[12,4096]{1,0:T(8,128)S(1)}, ...), condition=%wide.region_2.3_spmd.clone, body=%wide.region_0.2_spmd.clone.sunk | while | flops 3224637440 | bytes 991333 | solution.py:81
  9.5 3.1 %select_reduce_fusion.4 = f32[2,4096]{1,0:T(2,128)S(1)} fusion(pred[64,4096]{1,0:T(8,128)(4,1)S(1)} %iota_compare_fusion.14, f32[128,512]{1,0:T(8,128)S(1)} %get-tuple-element.265, s32[4096]{0:T(1024)S(1)} %bitcast.76), kind=kOutput, calls=%fused_computation.8.clone.1 | convolution fusion | flops 3224363008 | bytes 573440 | tf_op jit(solution)/shard_map/while/body/eval_jaxpr/dot_general | solution.py:69
  14.1 3.1 %select_reduce_fusion.4 = f32[2,4096]{1,0:T(2,128)S(1)} fusion(pred[64,4096]{1,0:T(8,128)(4,1)S(1)} %iota_compare_fusion.14, f32[128,512]{1,0:T(8,128)S(1)} %get-tuple-element.265, s32[4096]{0:T(1024)S(1)} %bitcast.76), kind=kOutput, calls=%fused_computation.8.clone.1 | convolution fusion | flops 3224363008 | bytes 573440 | tf_op jit(solution)/shard_map/while/body/eval_jaxpr/dot_general | solution.py:69
  18.6 3.1 %select_reduce_fusion.4 = f32[2,4096]{1,0:T(2,128)S(1)} fusion(pred[64,4096]{1,0:T(8,128)(4,1)S(1)} %iota_compare_fusion.14, f32[128,512]{1,0:T(8,128)S(1)} %get-tuple-element.265, s32[4096]{0:T(1024)S(1)} %bitcast.76), kind=kOutput, calls=%fused_computation.8.clone.1 | convolution fusion | flops 3224363008 | bytes 573440 | tf_op jit(solution)/shard_map/while/body/eval_jaxpr/dot_general | solution.py:69
  23.2 3.1 %select_reduce_fusion.4 = f32[2,4096]{1,0:T(2,128)S(1)} fusion(pred[64,4096]{1,0:T(8,128)(4,1)S(1)} %iota_compare_fusion.14, f32[128,512]{1,0:T(8,128)S(1)} %get-tuple-element.265, s32[4096]{0:T(1024)S(1)} %bitcast.76), kind=kOutput, calls=%fused_computation.8.clone.1 | convolution fusion | flops 3224363008 | bytes 573440 | tf_op jit(solution)/shard_map/while/body/eval_jaxpr/dot_general | solution.py:69
  27.7 3.1 %select_reduce_fusion.4 = f32[2,4096]{1,0:T(2,128)S(1)} fusion(pred[64,4096]{1,0:T(8,128)(4,1)S(1)} %iota_compare_fusion.14, f32[128,512]{1,0:T(8,128)S(1)} %get-tuple-element.265, s32[4096]{0:T(1024)S(1)} %bitcast.76), kind=kOutput, calls=%fused_computation.8.clone.1 | convolution fusion | flops 3224363008 | bytes 573440 | tf_op jit(solution)/shard_map/while/body/eval_jaxpr/dot_general | solution.py:69
  32.3 3.1 %select_reduce_fusion.4 = f32[2,4096]{1,0:T(2,128)S(1)} fusion(pred[64,4096]{1,0:T(8,128)(4,1)S(1)} %iota_compare_fusion.14, f32[128,512]{1,0:T(8,128)S(1)} %get-tuple-element.265, s32[4096]{0:T(1024)S(1)} %bitcast.76), kind=kOutput, calls=%fused_computation.8.clone.1 | convolution fusion | flops 3224363008 | bytes 573440 | tf_op jit(solution)/shard_map/while/body/eval_jaxpr/dot_general | solution.py:69
  36.8 3.1 %select_reduce_fusion.4 = f32[2,4096]{1,0:T(2,128)S(1)} fusion(pred[64,4096]{1,0:T(8,128)(4,1)S(1)} %iota_compare_fusion.14, f32[128,512]{1,0:T(8,128)S(1)} %get-tuple-element.265, s32[4096]{0:T(1024)S(1)} %bitcast.76), kind=kOutput, calls=%fused_computation.8.clone.1 | convolution fusion | flops 3224363008 | bytes 573440 | tf_op jit(solution)/shard_map/while/body/eval_jaxpr/dot_general | solution.py:69
  41.3 3.1 %select_reduce_fusion.4 = f32[2,4096]{1,0:T(2,128)S(1)} fusion(pred[64,4096]{1,0:T(8,128)(4,1)S(1)} %iota_compare_fusion.14, f32[128,512]{1,0:T(8,128)S(1)} %get-tuple-element.265, s32[4096]{0:T(1024)S(1)} %bitcast.76), kind=kOutput, calls=%fused_computation.8.clone.1 | convolution fusion | flops 3224363008 | bytes 573440 | tf_op jit(solution)/shard_map/while/body/eval_jaxpr/dot_general | solution.py:69
  45.9 3.1 %select_reduce_fusion.4 = f32[2,4096]{1,0:T(2,128)S(1)} fusion(pred[64,4096]{1,0:T(8,128)(4,1)S(1)} %iota_compare_fusion.14, f32[128,512]{1,0:T(8,128)S(1)} %get-tuple-element.265, s32[4096]{0:T(1024)S(1)} %bitcast.76), kind=kOutput, calls=%fused_computation.8.clone.1 | convolution fusion | flops 3224363008 | bytes 573440 | tf_op jit(solution)/shard_map/while/body/eval_jaxpr/dot_general | solution.py:69
  50.4 3.1 %select_reduce_fusion.4 = f32[2,4096]{1,0:T(2,128)S(1)} fusion(pred[64,4096]{1,0:T(8,128)(4,1)S(1)} %iota_compare_fusion.14, f32[128,512]{1,0:T(8,128)S(1)} %get-tuple-element.265, s32[4096]{0:T(1024)S(1)} %bitcast.76), kind=kOutput, calls=%fused_computation.8.clone.1 | convolution fusion | flops 3224363008 | bytes 573440 | tf_op jit(solution)/shard_map/while/body/eval_jaxpr/dot_general | solution.py:69
  55.0 3.1 %select_reduce_fusion.4 = f32[2,4096]{1,0:T(2,128)S(1)} fusion(pred[64,4096]{1,0:T(8,128)(4,1)S(1)} %iota_compare_fusion.14, f32[128,512]{1,0:T(8,128)S(1)} %get-tuple-element.265, s32[4096]{0:T(1024)S(1)} %bitcast.76), kind=kOutput, calls=%fused_computation.8.clone.1 | convolution fusion | flops 3224363008 | bytes 573440 | tf_op jit(solution)/shard_map/while/body/eval_jaxpr/dot_general | solution.py:69
  59.5 3.1 %select_reduce_fusion.4 = f32[2,4096]{1,0:T(2,128)S(1)} fusion(pred[64,4096]{1,0:T(8,128)(4,1)S(1)} %iota_compare_fusion.14, f32[128,512]{1,0:T(8,128)S(1)} %get-tuple-element.265, s32[4096]{0:T(1024)S(1)} %bitcast.76), kind=kOutput, calls=%fused_computation.8.clone.1 | convolution fusion | flops 3224363008 | bytes 573440 | tf_op jit(solution)/shard_map/while/body/eval_jaxpr/dot_general | solution.py:69
  65.3 1.8 %copy.20 = f32[2,32,4096]{2,0,1:T(2,128)} copy(f32[2,32,4096]{2,1,0:T(8,128)S(1)} %bitcast.71) | data formatting | bytes 2097152 | tf_op jit(solution)/shard_map/reshape | solution.py:88
  67.1 6.2 %all-to-all-start = ((f32[2,32,4096]{2,0,1:T(2,128)}), f32[2,32,4096]{2,0,1:T(2,128)S(1)}, u32[]{:S(2)}, u32[]{:S(2)}) async-start(f32[2,32,4096]{2,0,1:T(2,128)} %copy.20), calls=%async_computation | async-start | bytes 2097152 | tf_op jit(solution)/shard_map/all_to_all | solution.py:89
  73.4 1.6 constant_dynamic-update-slice_fusion.1
  76.0 1.9 %constant_dynamic-update-slice_fusion = f32[2,8,64,514]{3,2,1,0:T(8,128)} fusion(f32[2,8,64,514]{3,2,1,0:T(8,128)} %constant_dynamic-update-slice_fusion.1, f32[2,8,64,2]{3,2,1,0:T(8,128)} %collective-permute-done.1), kind=kLoop, calls=%fused_computation.45 | loop fusion | bytes 1048576 | tf_op jit(solution)/shard_map/concatenate | solution.py:19
  78.0 3.8 %multiply_add_fusion = f32[2,8,64,514]{3,2,1,0:T(8,128)S(1)} fusion(f32[2,8,64,514]{3,2,1,0:T(8,128)} %constant_dynamic-update-slice_fusion, f32[2,8,64,2]{3,2,1,0:T(8,128)} %collective-permute-done.1, f32[2,8,64,512]{3,2,1,0:T(8,128)S(1)} %copy-done, f32[2,8,64,2]{3,2,1,0:T(8,128)} %collective-permute-done, f32[8,64]{1,0:T(8,128)S(1)} %get-tuple-element.169, ...), kind=kLoop, calls=%fused_computation.30 | loop fusion | flops 5789696 | bytes 6328320 | tf_op jit(solution)/shard_map/add | solution.py:28
  82.4 1.3 multiply_add_fusion.1
  84.0 2.6 %pad_subtract_fusion.1 = f32[2,8,64,512]{3,2,1,0:T(8,128)} fusion(f32[2,7,64,512]{3,2,1,0:T(8,128)S(1)} %fusion.17, f32[8,64]{1,0:T(8,128)S(1)} %get-tuple-element.169, f32[2,8,64,514]{3,2,1,0:T(8,128)S(1)} %pad_subtract_fusion, f32[8,64]{1,0:T(8,128)S(1)} %get-tuple-element.168), kind=kLoop, calls=%fused_computation.33 | loop fusion | flops 5242880 | bytes 10227712 | tf_op jit(solution)/shard_map/sub | solution.py:38
  86.7 14.0 %all-to-all-done = f32[2,32,4096]{2,0,1:T(2,128)S(1)} async-done(((f32[2,32,4096]{2,0,1:T(2,128)}), f32[2,32,4096]{2,0,1:T(2,128)S(1)}, u32[]{:S(2)}, u32[]{:S(2)}) %all-to-all-start) | async-done | bytes 1048608 | tf_op jit(solution)/shard_map/all_to_all | solution.py:89
  101.3 1.0 select_reduce_fusion.1
  102.9 73.8 %while.24 = (s32[]{:T(128)}, f32[128,512]{1,0:T(8,128)S(1)}, s32[12,4096]{1,0:T(8,128)}, f32[12,2,4096]{2,1,0:T(2,128)S(1)}, s32[12,4096]{1,0:T(8,128)}, /*index=5*/s32[]{:T(128)}, s32[]{:T(128)}) while((s32[]{:T(128)}, f32[128,512]{1,0:T(8,128)S(1)}, s32[12,4096]{1,0:T(8,128)}, f32[12,2,4096]{2,1,0:T(2,128)S(1)}, ...), condition=%wide.region_6.7_spmd.clone, body=%wide.region_5.6_spmd.clone.sunk | while | flops 3224240128 | bytes 5439583 | solution.py:121
  102.9 1.1 constant_dynamic-slice_fusion.7
  104.3 4.7 %fusion.31 = f32[128,512]{1,0:T(8,128)S(1)} fusion(f32[128,4096]{1,0:T(8,128)S(1)} %bitcast.68, s32[4096]{0:T(1024)S(1)} %bitcast.75, f32[128,512]{1,0:T(8,128)S(1)} %get-tuple-element.275, pred[]{:T(512)S(6)} %compare.17), kind=kOutput, calls=%fused_computation.18.clone.1 | convolution fusion | flops 3223453696 | bytes 2637825 | tf_op jit(solution)/shard_map/while/body/eval_jaxpr/dot_general | solution.py:111
  109.1 1.0 constant_dynamic-slice_fusion.7
  110.5 4.7 %fusion.31 = f32[128,512]{1,0:T(8,128)S(1)} fusion(f32[128,4096]{1,0:T(8,128)S(1)} %bitcast.68, s32[4096]{0:T(1024)S(1)} %bitcast.75, f32[128,512]{1,0:T(8,128)S(1)} %get-tuple-element.275, pred[]{:T(512)S(6)} %compare.17), kind=kOutput, calls=%fused_computation.18.clone.1 | convolution fusion | flops 3223453696 | bytes 2637825 | tf_op jit(solution)/shard_map/while/body/eval_jaxpr/dot_general | solution.py:111
  115.2 1.0 constant_dynamic-slice_fusion.7
  116.6 4.7 %fusion.31 = f32[128,512]{1,0:T(8,128)S(1)} fusion(f32[128,4096]{1,0:T(8,128)S(1)} %bitcast.68, s32[4096]{0:T(1024)S(1)} %bitcast.75, f32[128,512]{1,0:T(8,128)S(1)} %get-tuple-element.275, pred[]{:T(512)S(6)} %compare.17), kind=kOutput, calls=%fused_computation.18.clone.1 | convolution fusion | flops 3223453696 | bytes 2637825 | tf_op jit(solution)/shard_map/while/body/eval_jaxpr/dot_general | solution.py:111
  121.4 1.0 constant_dynamic-slice_fusion.7
  122.8 4.7 %fusion.31 = f32[128,512]{1,0:T(8,128)S(1)} fusion(f32[128,4096]{1,0:T(8,128)S(1)} %bitcast.68, s32[4096]{0:T(1024)S(1)} %bitcast.75, f32[128,512]{1,0:T(8,128)S(1)} %get-tuple-element.275, pred[]{:T(512)S(6)} %compare.17), kind=kOutput, calls=%fused_computation.18.clone.1 | convolution fusion | flops 3223453696 | bytes 2637825 | tf_op jit(solution)/shard_map/while/body/eval_jaxpr/dot_general | solution.py:111
  127.5 1.0 constant_dynamic-slice_fusion.7
  128.9 4.7 %fusion.31 = f32[128,512]{1,0:T(8,128)S(1)} fusion(f32[128,4096]{1,0:T(8,128)S(1)} %bitcast.68, s32[4096]{0:T(1024)S(1)} %bitcast.75, f32[128,512]{1,0:T(8,128)S(1)} %get-tuple-element.275, pred[]{:T(512)S(6)} %compare.17), kind=kOutput, calls=%fused_computation.18.clone.1 | convolution fusion | flops 3223453696 | bytes 2637825 | tf_op jit(solution)/shard_map/while/body/eval_jaxpr/dot_general | solution.py:111
  133.7 1.0 constant_dynamic-slice_fusion.7
  135.1 4.7 %fusion.31 = f32[128,512]{1,0:T(8,128)S(1)} fusion(f32[128,4096]{1,0:T(8,128)S(1)} %bitcast.68, s32[4096]{0:T(1024)S(1)} %bitcast.75, f32[128,512]{1,0:T(8,128)S(1)} %get-tuple-element.275, pred[]{:T(512)S(6)} %compare.17), kind=kOutput, calls=%fused_computation.18.clone.1 | convolution fusion | flops 3223453696 | bytes 2637825 | tf_op jit(solution)/shard_map/while/body/eval_jaxpr/dot_general | solution.py:111
  139.8 1.0 constant_dynamic-slice_fusion.7
  141.2 4.7 %fusion.31 = f32[128,512]{1,0:T(8,128)S(1)} fusion(f32[128,4096]{1,0:T(8,128)S(1)} %bitcast.68, s32[4096]{0:T(1024)S(1)} %bitcast.75, f32[128,512]{1,0:T(8,128)S(1)} %get-tuple-element.275, pred[]{:T(512)S(6)} %compare.17), kind=kOutput, calls=%fused_computation.18.clone.1 | convolution fusion | flops 3223453696 | bytes 2637825 | tf_op jit(solution)/shard_map/while/body/eval_jaxpr/dot_general | solution.py:111
  146.0 1.0 constant_dynamic-slice_fusion.7
  147.3 4.7 %fusion.31 = f32[128,512]{1,0:T(8,128)S(1)} fusion(f32[128,4096]{1,0:T(8,128)S(1)} %bitcast.68, s32[4096]{0:T(1024)S(1)} %bitcast.75, f32[128,512]{1,0:T(8,128)S(1)} %get-tuple-element.275, pred[]{:T(512)S(6)} %compare.17), kind=kOutput, calls=%fused_computation.18.clone.1 | convolution fusion | flops 3223453696 | bytes 2637825 | tf_op jit(solution)/shard_map/while/body/eval_jaxpr/dot_general | solution.py:111
  152.1 1.0 constant_dynamic-slice_fusion.7
  153.5 4.7 %fusion.31 = f32[128,512]{1,0:T(8,128)S(1)} fusion(f32[128,4096]{1,0:T(8,128)S(1)} %bitcast.68, s32[4096]{0:T(1024)S(1)} %bitcast.75, f32[128,512]{1,0:T(8,128)S(1)} %get-tuple-element.275, pred[]{:T(512)S(6)} %compare.17), kind=kOutput, calls=%fused_computation.18.clone.1 | convolution fusion | flops 3223453696 | bytes 2637825 | tf_op jit(solution)/shard_map/while/body/eval_jaxpr/dot_general | solution.py:111
  158.3 1.0 constant_dynamic-slice_fusion.7
  159.6 4.7 %fusion.31 = f32[128,512]{1,0:T(8,128)S(1)} fusion(f32[128,4096]{1,0:T(8,128)S(1)} %bitcast.68, s32[4096]{0:T(1024)S(1)} %bitcast.75, f32[128,512]{1,0:T(8,128)S(1)} %get-tuple-element.275, pred[]{:T(512)S(6)} %compare.17), kind=kOutput, calls=%fused_computation.18.clone.1 | convolution fusion | flops 3223453696 | bytes 2637825 | tf_op jit(solution)/shard_map/while/body/eval_jaxpr/dot_general | solution.py:111
  165.8 4.7 %fusion.31 = f32[128,512]{1,0:T(8,128)S(1)} fusion(f32[128,4096]{1,0:T(8,128)S(1)} %bitcast.68, s32[4096]{0:T(1024)S(1)} %bitcast.75, f32[128,512]{1,0:T(8,128)S(1)} %get-tuple-element.275, pred[]{:T(512)S(6)} %compare.17), kind=kOutput, calls=%fused_computation.18.clone.1 | convolution fusion | flops 3223453696 | bytes 2637825 | tf_op jit(solution)/shard_map/while/body/eval_jaxpr/dot_general | solution.py:111
  171.9 4.7 %fusion.31 = f32[128,512]{1,0:T(8,128)S(1)} fusion(f32[128,4096]{1,0:T(8,128)S(1)} %bitcast.68, s32[4096]{0:T(1024)S(1)} %bitcast.75, f32[128,512]{1,0:T(8,128)S(1)} %get-tuple-element.275, pred[]{:T(512)S(6)} %compare.17), kind=kOutput, calls=%fused_computation.18.clone.1 | convolution fusion | flops 3223453696 | bytes 2637825 | tf_op jit(solution)/shard_map/while/body/eval_jaxpr/dot_general | solution.py:111
  176.7 1.1 add_bitcast_fusion
  (146 shorter events, 28.1 us)
Async XLA Ops:
  0.6 8.7 %slice-start = ((f32[2,8,64,512]{3,2,1,0:T(8,128)}), f32[2,1,64,512]{3,2,1,0:T(8,128)S(1)}, s32[]{:S(2)}) async-start(f32[2,8,64,512]{3,2,1,0:T(8,128)} %param.15), calls=%async_computation.1 | async-start | bytes 524288 | tf_op jit(solution)/shard_map/slice | solution.py:58
  0.6 8.4 %copy-start.5 = (s32[1,1,3,4,4096]{4,3,2,1,0:T(4,128)S(1)}, s32[1,1,3,4,4096]{4,3,2,1,0:T(4,128)}, u32[]{:S(2)}) copy-start(s32[1,1,3,4,4096]{4,3,2,1,0:T(4,128)} %param.21) | copy-start | bytes 589828
  0.7 8.5 %copy-start.6 = (s32[1,1,3,4,4096]{4,3,2,1,0:T(4,128)S(1)}, s32[1,1,3,4,4096]{4,3,2,1,0:T(4,128)}, u32[]{:S(2)}) copy-start(s32[1,1,3,4,4096]{4,3,2,1,0:T(4,128)} %param.22) | copy-start | bytes 589828
  0.7 8.6 %copy-start.11 = (s32[1,1,3,4]{3,1,2,0:T(1,128)S(1)}, s32[1,1,3,4]{3,1,2,0:T(1,128)}, u32[]{:S(2)}) copy-start(s32[1,1,3,4]{3,1,2,0:T(1,128)} %param.20) | copy-start | bytes 148
  3.1 73.0 %collective-permute-start.1 = (f32[2,8,64,2]{3,2,1,0:T(8,128)}, f32[2,8,64,2]{3,2,1,0:T(8,128)}, u32[]{:S(2)}, u32[]{:S(2)}) collective-permute-start(f32[2,8,64,2]{3,2,1,0:T(8,128)} %get-tuple-element.167), channel_id=1, source_target_pairs={{1,0},{2,1},{3,2},{4,3},{5,4},{6,5},{7,6},{0,7},{9,8},{10,9},{11,1... | collective-permute-start | bytes 24584 | tf_op jit(solution)/shard_map/ppermute | solution.py:18
  9.1 68.9 %collective-permute-start = (f32[2,8,64,2]{3,2,1,0:T(8,128)}, f32[2,8,64,2]{3,2,1,0:T(8,128)}, u32[]{:S(2)}, u32[]{:S(2)}) collective-permute-start(f32[2,8,64,2]{3,2,1,0:T(8,128)} %get-tuple-element.166), channel_id=1, source_target_pairs={{0,1},{1,2},{2,3},{3,4},{4,5},{5,6},{6,7},{7,0},{8,9},{9,10},{10,1... | collective-permute-start | bytes 24584 | tf_op jit(solution)/shard_map/ppermute | solution.py:15
  63.9 0.7 copy-start.1
  63.9 1.4 copy-start.2
  65.3 8.1 %copy-start.10 = (f32[8,64]{1,0:T(8,128)S(1)}, f32[8,64]{1,0:T(8,128)}, u32[]{:S(2)}) copy-start(f32[8,64]{1,0:T(8,128)} %param.16) | copy-start | bytes 6148
  65.3 8.1 %copy-start = (f32[2,8,64,512]{3,2,1,0:T(8,128)S(1)}, f32[2,8,64,512]{3,2,1,0:T(8,128)}, u32[]{:S(2)}) copy-start(f32[2,8,64,512]{3,2,1,0:T(8,128)} %param.15) | copy-start | bytes 6291460
  67.1 33.5 %all-to-all-start = ((f32[2,32,4096]{2,0,1:T(2,128)}), f32[2,32,4096]{2,0,1:T(2,128)S(1)}, u32[]{:S(2)}, u32[]{:S(2)}) async-start(f32[2,32,4096]{2,0,1:T(2,128)} %copy.20), calls=%async_computation | async-start | bytes 2097152 | tf_op jit(solution)/shard_map/all_to_all | solution.py:89
  78.0 3.8 %copy-start.9 = (f32[7,64]{1,0:T(8,128)S(1)}, f32[7,64]{1,0:T(8,128)}, u32[]{:S(2)}) copy-start(f32[7,64]{1,0:T(8,128)} %param.17) | copy-start | bytes 5380
  101.2 1.6 copy-start.3
  102.8 73.9 %copy-start.7 = (f32[64,512]{1,0:T(8,128)S(1)}, f32[64,512]{1,0:T(8,128)}, u32[]{:S(2)}) copy-start(f32[64,512]{1,0:T(8,128)} %param.18) | copy-start | bytes 393220
  102.9 73.9 %copy-start.8 = (s32[64,512]{1,0:T(8,128)S(1)}, s32[64,512]{1,0:T(8,128)}, u32[]{:S(2)}) copy-start(s32[64,512]{1,0:T(8,128)} %param.19) | copy-start | bytes 393220
  176.7 1.9 %copy-start.4 = (f32[128,512]{1,0:T(8,128)}, f32[128,512]{1,0:T(8,128)S(1)}, u32[]{:S(2)}) copy-start(f32[128,512]{1,0:T(8,128)S(1)} %get-tuple-element.99) | copy-start | bytes 786436
where the time goes:
time: 179 us
  matrix products  94.5 us (53%)
  local copies, waits for them, and re-layouts  30.5 us (17%)
  other arithmetic  25.3 us (14%)
  waiting for transfers between devices  14 us (8%)
  starting transfers between devices  12.2 us (7%)
    dot_general x12, matrix products, land_list(): lax.dot_general(spread, col_table, (((1,), (1,)), ((), ())), precision=la...  56.9 us
    dot_general x12, matrix products, pick_list(): jnp.dot(surface_rows, col_table, precision=lax.Precision.HIGHEST, preferr...  37.6 us
    dynamic_slice x36, local copies, waits for them, and re-layouts, shards(): unused, picked_all = lax.scan(pick_list, 0, (row_lists, col_lists, counts))  19.5 us
    all_to_all x1, waiting for transfers between devices, shards(): lax.all_to_all(blocks, ('comp', 'tile'), split_axis=1, concat_axis=1, til...  14 us
    lt x12, other arithmetic, pick_list(): values = jnp.where((slot_iota < count_one)[None, :], values, 0.0)  6.79 us
    all_to_all x1, starting transfers between devices, shards(): lax.all_to_all(blocks, ('comp', 'tile'), split_axis=1, concat_axis=1, til...  6.22 us
    ppermute x1, starting transfers between devices, with_halo(): lax.ppermute(lax.slice_in_dim(block, 0, width, axis=dim), axis, backward)  6 us
    add x2, other arithmetic, transport(): middle - 0.5 * speed * (right - left)  5.15 us
  transfers between devices with their start and end apart: 3, of which 1 were waited for; matrix products, arithmetic and copies ran while one was open for 39% of the time, Pallas kernels for 0%

commit v1 on v0

--- a/solution.py
+++ b/solution.py
@@ -1,9 +1,27 @@
+import functools
 import jax
 import jax.numpy as jnp
 from jax import lax
 from jax.sharding import PartitionSpec as P
+from jax.lax import all_to_all, axis_size
 
 SUBSTEPS = 2
+
+
+def place_corner(buf, dev_axis):
+    extra = jnp.concatenate(
+        all_to_all(
+            jnp.stack(jnp.split(buf, axis_size(dev_axis), axis=1)),
+            axis_name=dev_axis,
+            split_axis=0,
+            concat_axis=0,
+        ),
+        axis=1,
+    )
+    return extra
+
+
+_clear_tiles = functools.partial(place_corner, dev_axis=("comp", "tile"))
 
 
 def with_halo(block, sides, width):
@@ -86,7 +104,7 @@
     tile_table = partner_tiles[:, None] == jnp.arange(tile_total, dtype=jnp.int32)[None, :]
     spread = jnp.where(tile_table[None, :, None, :, None], outgoing[:, :, :, None, :], 0.0)
     blocks = jnp.sum(spread, axis=1).reshape(field_count, comp_peers * tile_total, slot_count)
-    arrived = lax.all_to_all(blocks, ("comp", "tile"), split_axis=1, concat_axis=1, tiled=True)
+    arrived = _clear_tiles(blocks)
     arrived = arrived.reshape(field_count, comp_peers, tile_total, slot_count)
     chosen = jnp.where(tile_table[None, :, None, :, None], arrived[:, None], 0.0)
     incoming = jnp.sum(chosen, axis=3)

time: 179 us -> 200 us (1.12)
  local copies, waits for them, and re-layouts: 30.5 us -> 50.6 us
    unnamed x25 -> x56, local copies, waits for them, and re-layouts: 2.4 us -> 21.9 us
  transfers between devices with their start and end apart: 3 -> 3, of which waited for: 1 -> 1; matrix products, arithmetic and copies ran while one was open for 39% -> 45% of each run, Pallas kernels for 0% -> 0%
where the time goes in v1:
time: 200 us; the launch traced here: 199 us
  matrix products  94.5 us (47%)
  local copies, waits for them, and re-layouts  50.6 us (25%)
  other arithmetic  26 us (13%)
  waiting for transfers between devices  13.9 us (7%)
  starting transfers between devices  12.2 us (6%)
    dot_general x12, matrix products, land_list(): lax.dot_general(spread, col_table, (((1,), (1,)), ((), ())), precision=la...  56.9 us
    dot_general x12, matrix products, pick_list(): jnp.dot(surface_rows, col_table, precision=lax.Precision.HIGHEST, preferr...  37.6 us
    unnamed x56, local copies, waits for them, and re-layouts  21.9 us
    dynamic_slice x36, local copies, waits for them, and re-layouts, shards(): unused, picked_all = lax.scan(pick_list, 0, (row_lists, col_lists, counts))  20.2 us
    all_to_all x1, waiting for transfers between devices, place_corner(): all_to_all(jnp.stack(jnp.split(buf, axis_size(dev_axis), axis=1)), axis_n...  13.9 us
    lt x12, other arithmetic, pick_list(): values = jnp.where((slot_iota < count_one)[None, :], values, 0.0)  7.5 us
    all_to_all x1, starting transfers between devices, place_corner(): all_to_all(jnp.stack(jnp.split(buf, axis_size(dev_axis), axis=1)), axis_n...  6.22 us
    ppermute x1, starting transfers between devices, with_halo(): lax.ppermute(lax.slice_in_dim(block, 0, width, axis=dim), axis, backward)  6 us
  transfers between devices with their start and end apart: 3, of which 1 were waited for; matrix products, arithmetic and copies ran while one was open for 45% of the time, Pallas kernels for 0%

profile of v1, /device:TPU:0, one launch (start us, length us, event | category | flops | bytes accessed | tf_op | source)
XLA Modules:
  0.0 199.3 jit_solution(7464765532289910595)
XLA Ops:
  0.7 2.4 %fusion.21 = (f32[2,8,64,2]{3,2,1,0:T(8,128)}, f32[2,8,64,2]{3,2,1,0:T(8,128)}) fusion(f32[2,8,64,512]{3,2,1,0:T(8,128)} %param.15), kind=kLoop, calls=%fused_computation.118 | loop fusion | bytes 32768 | tf_op jit(solution)/shard_map/slice | solution.py:34
  3.1 6.0 %collective-permute-start.1 = (f32[2,8,64,2]{3,2,1,0:T(8,128)}, f32[2,8,64,2]{3,2,1,0:T(8,128)}, u32[]{:S(2)}, u32[]{:S(2)}) collective-permute-start(f32[2,8,64,2]{3,2,1,0:T(8,128)} %get-tuple-element.167), channel_id=1, source_target_pairs={{1,0},{2,1},{3,2},{4,3},{5,4},{6,5},{7,6},{0,7},{9,8},{10,9},{11,1... | collective-permute-start | bytes 24584 | tf_op jit(solution)/shard_map/ppermute | solution.py:36
  9.4 55.9 %while.23 = (s32[]{:T(128)}, f32[12,2,4096]{2,1,0:T(2,128)S(1)}, s32[12]{0:T(128)S(1)}, s32[12,4096]{1,0:T(8,128)S(1)}, s32[12,4096]{1,0:T(8,128)S(1)}, /*index=5*/f32[128,512]{1,0:T(8,128)S(1)}, s32[]{:T(128)}) while((s32[]{:T(128)}, f32[12,2,4096]{2,1,0:T(2,128)S(1)}, s32[12]{0:T(128)S(1)}, s32[12,4096]{1,0:T(8,128)S(1)}, ...), condition=%wide.region_2.3_spmd.clone, body=%wide.region_0.2_spmd.clone.sunk | while | flops 3224637440 | bytes 991341 | solution.py:99
  9.6 3.1 %select_reduce_fusion.4 = f32[2,4096]{1,0:T(2,128)S(1)} fusion(pred[64,4096]{1,0:T(8,128)(4,1)S(1)} %iota_compare_fusion.14, f32[128,512]{1,0:T(8,128)S(1)} %get-tuple-element.297, s32[4096]{0:T(1024)S(1)} %bitcast.207), kind=kOutput, calls=%fused_computation.8.clone.1 | convolution fusion | flops 3224363008 | bytes 573440 | tf_op jit(solution)/shard_map/while/body/eval_jaxpr/dot_general | solution.py:87
  14.2 3.1 %select_reduce_fusion.4 = f32[2,4096]{1,0:T(2,128)S(1)} fusion(pred[64,4096]{1,0:T(8,128)(4,1)S(1)} %iota_compare_fusion.14, f32[128,512]{1,0:T(8,128)S(1)} %get-tuple-element.297, s32[4096]{0:T(1024)S(1)} %bitcast.207), kind=kOutput, calls=%fused_computation.8.clone.1 | convolution fusion | flops 3224363008 | bytes 573440 | tf_op jit(solution)/shard_map/while/body/eval_jaxpr/dot_general | solution.py:87
  18.9 3.1 %select_reduce_fusion.4 = f32[2,4096]{1,0:T(2,128)S(1)} fusion(pred[64,4096]{1,0:T(8,128)(4,1)S(1)} %iota_compare_fusion.14, f32[128,512]{1,0:T(8,128)S(1)} %get-tuple-element.297, s32[4096]{0:T(1024)S(1)} %bitcast.207), kind=kOutput, calls=%fused_computation.8.clone.1 | convolution fusion | flops 3224363008 | bytes 573440 | tf_op jit(solution)/shard_map/while/body/eval_jaxpr/dot_general | solution.py:87
  23.5 3.1 %select_reduce_fusion.4 = f32[2,4096]{1,0:T(2,128)S(1)} fusion(pred[64,4096]{1,0:T(8,128)(4,1)S(1)} %iota_compare_fusion.14, f32[128,512]{1,0:T(8,128)S(1)} %get-tuple-element.297, s32[4096]{0:T(1024)S(1)} %bitcast.207), kind=kOutput, calls=%fused_computation.8.clone.1 | convolution fusion | flops 3224363008 | bytes 573440 | tf_op jit(solution)/shard_map/while/body/eval_jaxpr/dot_general | solution.py:87
  28.2 3.1 %select_reduce_fusion.4 = f32[2,4096]{1,0:T(2,128)S(1)} fusion(pred[64,4096]{1,0:T(8,128)(4,1)S(1)} %iota_compare_fusion.14, f32[128,512]{1,0:T(8,128)S(1)} %get-tuple-element.297, s32[4096]{0:T(1024)S(1)} %bitcast.207), kind=kOutput, calls=%fused_computation.8.clone.1 | convolution fusion | flops 3224363008 | bytes 573440 | tf_op jit(solution)/shard_map/while/body/eval_jaxpr/dot_general | solution.py:87
  32.9 3.1 %select_reduce_fusion.4 = f32[2,4096]{1,0:T(2,128)S(1)} fusion(pred[64,4096]{1,0:T(8,128)(4,1)S(1)} %iota_compare_fusion.14, f32[128,512]{1,0:T(8,128)S(1)} %get-tuple-element.297, s32[4096]{0:T(1024)S(1)} %bitcast.207), kind=kOutput, calls=%fused_computation.8.clone.1 | convolution fusion | flops 3224363008 | bytes 573440 | tf_op jit(solution)/shard_map/while/body/eval_jaxpr/dot_general | solution.py:87
  37.5 3.1 %select_reduce_fusion.4 = f32[2,4096]{1,0:T(2,128)S(1)} fusion(pred[64,4096]{1,0:T(8,128)(4,1)S(1)} %iota_compare_fusion.14, f32[128,512]{1,0:T(8,128)S(1)} %get-tuple-element.297, s32[4096]{0:T(1024)S(1)} %bitcast.207), kind=kOutput, calls=%fused_computation.8.clone.1 | convolution fusion | flops 3224363008 | bytes 573440 | tf_op jit(solution)/shard_map/while/body/eval_jaxpr/dot_general | solution.py:87
  42.2 3.1 %select_reduce_fusion.4 = f32[2,4096]{1,0:T(2,128)S(1)} fusion(pred[64,4096]{1,0:T(8,128)(4,1)S(1)} %iota_compare_fusion.14, f32[128,512]{1,0:T(8,128)S(1)} %get-tuple-element.297, s32[4096]{0:T(1024)S(1)} %bitcast.207), kind=kOutput, calls=%fused_computation.8.clone.1 | convolution fusion | flops 3224363008 | bytes 573440 | tf_op jit(solution)/shard_map/while/body/eval_jaxpr/dot_general | solution.py:87
  46.8 3.1 %select_reduce_fusion.4 = f32[2,4096]{1,0:T(2,128)S(1)} fusion(pred[64,4096]{1,0:T(8,128)(4,1)S(1)} %iota_compare_fusion.14, f32[128,512]{1,0:T(8,128)S(1)} %get-tuple-element.297, s32[4096]{0:T(1024)S(1)} %bitcast.207), kind=kOutput, calls=%fused_computation.8.clone.1 | convolution fusion | flops 3224363008 | bytes 573440 | tf_op jit(solution)/shard_map/while/body/eval_jaxpr/dot_general | solution.py:87
  51.5 3.1 %select_reduce_fusion.4 = f32[2,4096]{1,0:T(2,128)S(1)} fusion(pred[64,4096]{1,0:T(8,128)(4,1)S(1)} %iota_compare_fusion.14, f32[128,512]{1,0:T(8,128)S(1)} %get-tuple-element.297, s32[4096]{0:T(1024)S(1)} %bitcast.207), kind=kOutput, calls=%fused_computation.8.clone.1 | convolution fusion | flops 3224363008 | bytes 573440 | tf_op jit(solution)/shard_map/while/body/eval_jaxpr/dot_general | solution.py:87
  56.2 3.1 %select_reduce_fusion.4 = f32[2,4096]{1,0:T(2,128)S(1)} fusion(pred[64,4096]{1,0:T(8,128)(4,1)S(1)} %iota_compare_fusion.14, f32[128,512]{1,0:T(8,128)S(1)} %get-tuple-element.297, s32[4096]{0:T(1024)S(1)} %bitcast.207), kind=kOutput, calls=%fused_computation.8.clone.1 | convolution fusion | flops 3224363008 | bytes 573440 | tf_op jit(solution)/shard_map/while/body/eval_jaxpr/dot_general | solution.py:87
  60.8 3.1 %select_reduce_fusion.4 = f32[2,4096]{1,0:T(2,128)S(1)} fusion(pred[64,4096]{1,0:T(8,128)(4,1)S(1)} %iota_compare_fusion.14, f32[128,512]{1,0:T(8,128)S(1)} %get-tuple-element.297, s32[4096]{0:T(1024)S(1)} %bitcast.207), kind=kOutput, calls=%fused_computation.8.clone.1 | convolution fusion | flops 3224363008 | bytes 573440 | tf_op jit(solution)/shard_map/while/body/eval_jaxpr/dot_general | solution.py:87
  87.8 6.2 %all-to-all-start = ((f32[32,2,1,4096]{3,1,2,0:T(2,128)}), f32[32,2,1,4096]{3,1,2,0:T(2,128)S(1)}, u32[]{:S(2)}, u32[]{:S(2)}) async-start(f32[32,2,1,4096]{3,1,2,0:T(2,128)} %constant_dynamic-update-slice_fusion.2), calls=%async_computation | async-start | bytes 2097152 | tf_op jit(solution)/shard_map/all_to_all | solution.py:13
  94.1 1.7 constant_dynamic-update-slice_fusion.1
  96.8 1.9 constant_dynamic-update-slice_fusion
  98.7 3.8 %multiply_add_fusion = f32[2,8,64,514]{3,2,1,0:T(8,128)S(1)} fusion(f32[2,8,64,514]{3,2,1,0:T(8,128)} %constant_dynamic-update-slice_fusion, f32[2,8,64,2]{3,2,1,0:T(8,128)} %collective-permute-done.1, f32[2,8,64,512]{3,2,1,0:T(8,128)S(1)} %copy-done, f32[2,8,64,2]{3,2,1,0:T(8,128)} %collective-permute-done, f32[8,64]{1,0:T(8,128)S(1)} %get-tuple-element.201, ...), kind=kLoop, calls=%fused_computation.30 | loop fusion | flops 5789696 | bytes 6328320 | tf_op jit(solution)/shard_map/add | solution.py:46
  103.2 1.3 multiply_add_fusion.1
  104.8 2.6 %pad_subtract_fusion.1 = f32[2,8,64,512]{3,2,1,0:T(8,128)} fusion(f32[2,7,64,512]{3,2,1,0:T(8,128)S(1)} %fusion.17, f32[8,64]{1,0:T(8,128)S(1)} %get-tuple-element.201, f32[2,8,64,514]{3,2,1,0:T(8,128)S(1)} %pad_subtract_fusion, f32[8,64]{1,0:T(8,128)S(1)} %get-tuple-element.200), kind=kLoop, calls=%fused_computation.33 | loop fusion | flops 5242880 | bytes 10227712 | tf_op jit(solution)/shard_map/sub | solution.py:56
  107.4 13.9 %all-to-all-done = f32[32,2,1,4096]{3,1,2,0:T(2,128)S(1)} async-done(((f32[32,2,1,4096]{3,1,2,0:T(2,128)}), f32[32,2,1,4096]{3,1,2,0:T(2,128)S(1)}, u32[]{:S(2)}, u32[]{:S(2)}) %all-to-all-start) | async-done | bytes 1048608 | tf_op jit(solution)/shard_map/all_to_all | solution.py:13
  122.0 1.0 select_reduce_fusion.1
  123.6 73.8 %while.24 = (s32[]{:T(128)}, f32[128,512]{1,0:T(8,128)S(1)}, s32[12,4096]{1,0:T(8,128)}, f32[12,2,4096]{2,1,0:T(2,128)S(1)}, s32[12,4096]{1,0:T(8,128)}, /*index=5*/s32[]{:T(128)}, s32[]{:T(128)}) while((s32[]{:T(128)}, f32[128,512]{1,0:T(8,128)S(1)}, s32[12,4096]{1,0:T(8,128)}, f32[12,2,4096]{2,1,0:T(2,128)S(1)}, ...), condition=%wide.region_6.7_spmd.clone, body=%wide.region_5.6_spmd.clone.sunk | while | flops 3224240128 | bytes 5439591 | solution.py:139
  123.6 1.1 constant_dynamic-slice_fusion.7
  125.1 4.7 %fusion.33 = f32[128,512]{1,0:T(8,128)S(1)} fusion(f32[128,4096]{1,0:T(8,128)S(1)} %bitcast.198, s32[4096]{0:T(1024)S(1)} %bitcast.206, f32[128,512]{1,0:T(8,128)S(1)} %get-tuple-element.307, pred[]{:T(512)S(6)} %compare.17), kind=kOutput, calls=%fused_computation.18.clone.1 | convolution fusion | flops 3223453696 | bytes 2637825 | tf_op jit(solution)/shard_map/while/body/eval_jaxpr/dot_general | solution.py:129
  129.8 1.0 constant_dynamic-slice_fusion.7
  131.2 4.7 %fusion.33 = f32[128,512]{1,0:T(8,128)S(1)} fusion(f32[128,4096]{1,0:T(8,128)S(1)} %bitcast.198, s32[4096]{0:T(1024)S(1)} %bitcast.206, f32[128,512]{1,0:T(8,128)S(1)} %get-tuple-element.307, pred[]{:T(512)S(6)} %compare.17), kind=kOutput, calls=%fused_computation.18.clone.1 | convolution fusion | flops 3223453696 | bytes 2637825 | tf_op jit(solution)/shard_map/while/body/eval_jaxpr/dot_general | solution.py:129
  136.0 1.0 constant_dynamic-slice_fusion.7
  137.4 4.7 %fusion.33 = f32[128,512]{1,0:T(8,128)S(1)} fusion(f32[128,4096]{1,0:T(8,128)S(1)} %bitcast.198, s32[4096]{0:T(1024)S(1)} %bitcast.206, f32[128,512]{1,0:T(8,128)S(1)} %get-tuple-element.307, pred[]{:T(512)S(6)} %compare.17), kind=kOutput, calls=%fused_computation.18.clone.1 | convolution fusion | flops 3223453696 | bytes 2637825 | tf_op jit(solution)/shard_map/while/body/eval_jaxpr/dot_general | solution.py:129
  142.1 1.0 constant_dynamic-slice_fusion.7
  143.5 4.7 %fusion.33 = f32[128,512]{1,0:T(8,128)S(1)} fusion(f32[128,4096]{1,0:T(8,128)S(1)} %bitcast.198, s32[4096]{0:T(1024)S(1)} %bitcast.206, f32[128,512]{1,0:T(8,128)S(1)} %get-tuple-element.307, pred[]{:T(512)S(6)} %compare.17), kind=kOutput, calls=%fused_computation.18.clone.1 | convolution fusion | flops 3223453696 | bytes 2637825 | tf_op jit(solution)/shard_map/while/body/eval_jaxpr/dot_general | solution.py:129
  148.3 1.0 constant_dynamic-slice_fusion.7
  149.7 4.7 %fusion.33 = f32[128,512]{1,0:T(8,128)S(1)} fusion(f32[128,4096]{1,0:T(8,128)S(1)} %bitcast.198, s32[4096]{0:T(1024)S(1)} %bitcast.206, f32[128,512]{1,0:T(8,128)S(1)} %get-tuple-element.307, pred[]{:T(512)S(6)} %compare.17), kind=kOutput, calls=%fused_computation.18.clone.1 | convolution fusion | flops 3223453696 | bytes 2637825 | tf_op jit(solution)/shard_map/while/body/eval_jaxpr/dot_general | solution.py:129
  154.4 1.0 constant_dynamic-slice_fusion.7
  155.8 4.7 %fusion.33 = f32[128,512]{1,0:T(8,128)S(1)} fusion(f32[128,4096]{1,0:T(8,128)S(1)} %bitcast.198, s32[4096]{0:T(1024)S(1)} %bitcast.206, f32[128,512]{1,0:T(8,128)S(1)} %get-tuple-element.307, pred[]{:T(512)S(6)} %compare.17), kind=kOutput, calls=%fused_computation.18.clone.1 | convolution fusion | flops 3223453696 | bytes 2637825 | tf_op jit(solution)/shard_map/while/body/eval_jaxpr/dot_general | solution.py:129
  160.6 1.0 constant_dynamic-slice_fusion.7
  161.9 4.7 %fusion.33 = f32[128,512]{1,0:T(8,128)S(1)} fusion(f32[128,4096]{1,0:T(8,128)S(1)} %bitcast.198, s32[4096]{0:T(1024)S(1)} %bitcast.206, f32[128,512]{1,0:T(8,128)S(1)} %get-tuple-element.307, pred[]{:T(512)S(6)} %compare.17), kind=kOutput, calls=%fused_computation.18.clone.1 | convolution fusion | flops 3223453696 | bytes 2637825 | tf_op jit(solution)/shard_map/while/body/eval_jaxpr/dot_general | solution.py:129
  166.7 1.0 constant_dynamic-slice_fusion.7
  168.1 4.7 %fusion.33 = f32[128,512]{1,0:T(8,128)S(1)} fusion(f32[128,4096]{1,0:T(8,128)S(1)} %bitcast.198, s32[4096]{0:T(1024)S(1)} %bitcast.206, f32[128,512]{1,0:T(8,128)S(1)} %get-tuple-element.307, pred[]{:T(512)S(6)} %compare.17), kind=kOutput, calls=%fused_computation.18.clone.1 | convolution fusion | flops 3223453696 | bytes 2637825 | tf_op jit(solution)/shard_map/while/body/eval_jaxpr/dot_general | solution.py:129
  172.9 1.0 constant_dynamic-slice_fusion.7
  174.2 4.7 %fusion.33 = f32[128,512]{1,0:T(8,128)S(1)} fusion(f32[128,4096]{1,0:T(8,128)S(1)} %bitcast.198, s32[4096]{0:T(1024)S(1)} %bitcast.206, f32[128,512]{1,0:T(8,128)S(1)} %get-tuple-element.307, pred[]{:T(512)S(6)} %compare.17), kind=kOutput, calls=%fused_computation.18.clone.1 | convolution fusion | flops 3223453696 | bytes 2637825 | tf_op jit(solution)/shard_map/while/body/eval_jaxpr/dot_general | solution.py:129
  179.0 1.0 constant_dynamic-slice_fusion.7
  180.4 4.7 %fusion.33 = f32[128,512]{1,0:T(8,128)S(1)} fusion(f32[128,4096]{1,0:T(8,128)S(1)} %bitcast.198, s32[4096]{0:T(1024)S(1)} %bitcast.206, f32[128,512]{1,0:T(8,128)S(1)} %get-tuple-element.307, pred[]{:T(512)S(6)} %compare.17), kind=kOutput, calls=%fused_computation.18.clone.1 | convolution fusion | flops 3223453696 | bytes 2637825 | tf_op jit(solution)/shard_map/while/body/eval_jaxpr/dot_general | solution.py:129
  185.2 1.0 constant_dynamic-slice_fusion.7
  186.5 4.7 %fusion.33 = f32[128,512]{1,0:T(8,128)S(1)} fusion(f32[128,4096]{1,0:T(8,128)S(1)} %bitcast.198, s32[4096]{0:T(1024)S(1)} %bitcast.206, f32[128,512]{1,0:T(8,128)S(1)} %get-tuple-element.307, pred[]{:T(512)S(6)} %compare.17), kind=kOutput, calls=%fused_computation.18.clone.1 | convolution fusion | flops 3223453696 | bytes 2637825 | tf_op jit(solution)/shard_map/while/body/eval_jaxpr/dot_general | solution.py:129
  192.7 4.7 %fusion.33 = f32[128,512]{1,0:T(8,128)S(1)} fusion(f32[128,4096]{1,0:T(8,128)S(1)} %bitcast.198, s32[4096]{0:T(1024)S(1)} %bitcast.206, f32[128,512]{1,0:T(8,128)S(1)} %get-tuple-element.307, pred[]{:T(512)S(6)} %compare.17), kind=kOutput, calls=%fused_computation.18.clone.1 | convolution fusion | flops 3223453696 | bytes 2637825 | tf_op jit(solution)/shard_map/while/body/eval_jaxpr/dot_general | solution.py:129
  197.5 1.1 add_bitcast_fusion
  (179 shorter events, 49.6 us)
Async XLA Ops:
  0.6 8.7 %slice-start = ((f32[2,8,64,512]{3,2,1,0:T(8,128)}), f32[2,1,64,512]{3,2,1,0:T(8,128)S(1)}, s32[]{:S(2)}) async-start(f32[2,8,64,512]{3,2,1,0:T(8,128)} %param.15), calls=%async_computation.1 | async-start | bytes 524288 | tf_op jit(solution)/shard_map/slice | solution.py:76
  0.6 8.4 %copy-start.5 = (s32[1,1,3,4,4096]{4,3,2,1,0:T(4,128)S(1)}, s32[1,1,3,4,4096]{4,3,2,1,0:T(4,128)}, u32[]{:S(2)}) copy-start(s32[1,1,3,4,4096]{4,3,2,1,0:T(4,128)} %param.21) | copy-start | bytes 589828
  0.7 8.5 %copy-start.11 = (s32[1,1,3,4]{3,1,2,0:T(1,128)S(1)}, s32[1,1,3,4]{3,1,2,0:T(1,128)}, u32[]{:S(2)}) copy-start(s32[1,1,3,4]{3,1,2,0:T(1,128)} %param.20) | copy-start | bytes 148
  0.7 8.6 %copy-start.6 = (s32[1,1,3,4,4096]{4,3,2,1,0:T(4,128)S(1)}, s32[1,1,3,4,4096]{4,3,2,1,0:T(4,128)}, u32[]{:S(2)}) copy-start(s32[1,1,3,4,4096]{4,3,2,1,0:T(4,128)} %param.22) | copy-start | bytes 589828
  3.1 93.7 %collective-permute-start.1 = (f32[2,8,64,2]{3,2,1,0:T(8,128)}, f32[2,8,64,2]{3,2,1,0:T(8,128)}, u32[]{:S(2)}, u32[]{:S(2)}) collective-permute-start(f32[2,8,64,2]{3,2,1,0:T(8,128)} %get-tuple-element.167), channel_id=1, source_target_pairs={{1,0},{2,1},{3,2},{4,3},{5,4},{6,5},{7,6},{0,7},{9,8},{10,9},{11,1... | collective-permute-start | bytes 24584 | tf_op jit(solution)/shard_map/ppermute | solution.py:36
  9.1 89.7 %collective-permute-start = (f32[2,8,64,2]{3,2,1,0:T(8,128)}, f32[2,8,64,2]{3,2,1,0:T(8,128)}, u32[]{:S(2)}, u32[]{:S(2)}) collective-permute-start(f32[2,8,64,2]{3,2,1,0:T(8,128)} %get-tuple-element.166), channel_id=1, source_target_pairs={{0,1},{1,2},{2,3},{3,4},{4,5},{5,6},{6,7},{7,0},{8,9},{9,10},{10,1... | collective-permute-start | bytes 24584 | tf_op jit(solution)/shard_map/ppermute | solution.py:33
  65.3 0.7 copy-start.1
  65.3 2.4 %copy-start.2 = (s32[12,4096]{1,0:T(8,128)}, s32[12,4096]{1,0:T(8,128)S(1)}, u32[]{:S(2)}) copy-start(s32[12,4096]{1,0:T(8,128)S(1)} %get-tuple-element.322) | copy-start | bytes 589828
  68.4 25.7 %copy-start.10 = (f32[8,64]{1,0:T(8,128)S(1)}, f32[8,64]{1,0:T(8,128)}, u32[]{:S(2)}) copy-start(f32[8,64]{1,0:T(8,128)} %param.16) | copy-start | bytes 6148
  68.4 25.7 %copy-start = (f32[2,8,64,512]{3,2,1,0:T(8,128)S(1)}, f32[2,8,64,512]{3,2,1,0:T(8,128)}, u32[]{:S(2)}) copy-start(f32[2,8,64,512]{3,2,1,0:T(8,128)} %param.15) | copy-start | bytes 6291460
  87.8 33.5 %all-to-all-start = ((f32[32,2,1,4096]{3,1,2,0:T(2,128)}), f32[32,2,1,4096]{3,1,2,0:T(2,128)S(1)}, u32[]{:S(2)}, u32[]{:S(2)}) async-start(f32[32,2,1,4096]{3,1,2,0:T(2,128)} %constant_dynamic-update-slice_fusion.2), calls=%async_computation | async-start | bytes 2097152 | tf_op jit(solution)/shard_map/all_to_all | solution.py:13
  98.7 3.8 %copy-start.9 = (f32[7,64]{1,0:T(8,128)S(1)}, f32[7,64]{1,0:T(8,128)}, u32[]{:S(2)}) copy-start(f32[7,64]{1,0:T(8,128)} %param.17) | copy-start | bytes 5380
  122.0 1.6 copy-start.3
  123.6 73.9 %copy-start.7 = (f32[64,512]{1,0:T(8,128)S(1)}, f32[64,512]{1,0:T(8,128)}, u32[]{:S(2)}) copy-start(f32[64,512]{1,0:T(8,128)} %param.18) | copy-start | bytes 393220
  123.6 73.9 %copy-start.8 = (s32[64,512]{1,0:T(8,128)S(1)}, s32[64,512]{1,0:T(8,128)}, u32[]{:S(2)}) copy-start(s32[64,512]{1,0:T(8,128)} %param.19) | copy-start | bytes 393220
  197.4 1.9 copy-start.4
